TPU v7x, 32 devices: a whole 2x2x4 slice. The times are simulated.
32 devices in a mesh: slab: 4 (over x, core), panel: 8 (over z, y).
Axes of the slice: x: 2, y: 2, z: 4, core: 2. Of those that a mesh axis runs over, the one named last changes fastest.
Arguments:
- ranges: float32 [4, 4, 1024, 1024], P('slab', None, 'panel'), may hold values from -1.5 to 1.5
- pattern: int32 [4, 4, 16, 16], P('slab'), may hold values 0 or 1
Outputs:
- combined: float32 [4, 4, 1024, 1024], P('slab', None, 'panel')
All inputs are finite; a program needn't handle non-finite values. No bound on the sum of `pattern` on one device may be relied on, other than what follows from the above.
Results may differ from a plain program's by a relative error of at most 0.01.
Values may be sent and summed in bfloat16 or wider, within the bound.
A program may use at most 64 MiB of HBM per device.

v0:
```python
import jax
import jax.numpy as jnp
from jax import lax
from jax.sharding import PartitionSpec as P

M = 1024
BLK = 64
LEVELS = 2


def partner_2(block, axis, distance):
    count = lax.axis_size(axis)
    route = []
    for low in range(count):
        high = low | 1 << distance
        if high != low and high < count:
            route += [(low, high), (high, low)]
    return lax.ppermute(block, axis, route)


def to_half(values):
    return values.astype(jnp.bfloat16)


def star(head, tail, tree_level, row_start):
    head_top, head_up, head_down, head_bottom = (head[0], head[1], head[2], head[3])
    tail_top, tail_up, tail_down, tail_bottom = (tail[0], tail[1], tail[2], tail[3])
    local_rows = head.shape[1]
    col_side = lax.axis_index("slab") >> tree_level & 1
    col_start = col_side * (M // 2)

    def cut_cols(values):
        return lax.dynamic_slice_in_dim(to_half(values), col_start, M // 2, 1)

    right_bottom, right_up, right_down = (
        lax.all_gather(cut_cols(head_bottom), "panel", axis=0, tiled=True),
        lax.all_gather(cut_cols(tail_up), "panel", axis=0, tiled=True),
        lax.all_gather(cut_cols(head_down), "panel", axis=0, tiled=True),
    )

    def spread(values):
        return lax.all_gather(cut_cols(values), "panel", axis=0, tiled=True)

    def multiply(left, right):
        half_cols = jnp.dot(to_half(left), right, preferred_element_type=jnp.float32)
        other_cols = partner_2(half_cols, "slab", tree_level)
        return jnp.where(
            col_side == 0,
            jnp.concatenate([half_cols, other_cols], 1),
            jnp.concatenate([other_cols, half_cols], 1),
        )

    col_ids = col_start + jnp.arange(M // 2, dtype=jnp.int32)
    all_ids = jnp.arange(M, dtype=jnp.int32)
    eye_right = (all_ids[:, None] == col_ids[None, :]).astype(jnp.float32)
    row_ids = row_start + jnp.arange(local_rows, dtype=jnp.int32)
    eye_rows = (row_ids[:, None] == all_ids[None, :]).astype(jnp.float32)
    loop_term = multiply(tail_top, right_bottom)
    loop_kept = lax.optimization_barrier(to_half(loop_term)).astype(jnp.float32)
    right_loop = spread(loop_term)
    right_defect = to_half(eye_right - right_loop.astype(jnp.float32))
    right_guess = to_half(eye_right + right_loop.astype(jnp.float32))
    guess = eye_rows + loop_kept
    guess = 2.0 * guess - multiply(multiply(guess, right_defect), right_guess)
    right_inverse = spread(guess)
    lifted = multiply(head_up, right_inverse)
    joint_up = multiply(lifted, right_up)
    bounce = multiply(tail_top, right_down)
    right_bounce = spread(bounce)
    joint_top = head_top + multiply(lifted, right_bounce)
    reach = multiply(tail_down, right_bottom)
    through = multiply(reach, right_inverse)
    joint_down = multiply(tail_down, right_down) + multiply(through, right_bounce)
    joint_bottom = (
        tail_bottom + multiply(reach, right_up) + multiply(multiply(through, right_loop), right_up)
    )
    return jnp.stack([joint_top, joint_up, joint_down, joint_bottom])


def body(ranges, pattern):
    group_blocks = ranges[0]
    local_rows = group_blocks.shape[1]
    block_count = pattern.shape[2]
    row_start = lax.axis_index("panel") * local_rows
    row_ids = row_start + jnp.arange(local_rows, dtype=jnp.int32)
    col_ids = jnp.arange(M, dtype=jnp.int32)
    block_ids = jnp.arange(block_count, dtype=jnp.int32)
    row_pick = (row_ids[:, None] // BLK == block_ids[None, :]).astype(jnp.float32)
    col_pick = (block_ids[:, None] == col_ids[None, :] // BLK).astype(jnp.float32)
    block_mask = jnp.einsum("mi,gij,jc->gmc", row_pick, pattern[0].astype(jnp.float32), col_pick)
    merged = group_blocks * block_mask
    for tree_level in range(LEVELS):
        partner = partner_2(merged, "slab", tree_level)
        is_lower = lax.axis_index("slab") >> tree_level & 1 == 0
        head_blocks = jnp.where(is_lower, merged, partner)
        tail_blocks = jnp.where(is_lower, partner, merged)
        merged = star(head_blocks, tail_blocks, tree_level, row_start)
    return merged[None]


def solution(mesh):
    return jax.shard_map(
        body,
        mesh=mesh,
        in_specs=(P("slab", None, "panel", None), P("slab", None, None, None)),
        out_specs=P("slab", None, "panel", None),
        check_vma=False,
    )
```

profile of v0, /device:TPU:0, one launch (start us, length us, event | category | flops | bytes accessed | tf_op | source)
XLA Modules:
  0.0 616.8 jit_solution(5166546670370426008)
XLA Ops:
  6.6 2.3 bitcast_multiply_fusion
  9.4 3.9 collective-permute-done
  13.3 4.4 fusion.131
  19.5 43.0 %all-gather.31.cloned.1.call-done = bf16[1,1024,512]{2,1,0:T(8,128)(2,1)} async-done(((bf16[1,128,512]{2,1,0:T(8,128)(2,1)}), bf16[1,1024,512]{2,1,0:T(8,128)(2,1)}) %all-gather.31.cloned.1.call-update) | async-done | bytes 1048592 | tf_op jit(solution)/shard_map/all_gather | solution.py:36
  67.8 37.5 %all-gather.19.cloned.1.call-done = bf16[1024,512]{1,0:T(8,128)(2,1)} async-done(((bf16[128,512]{1,0:T(8,128)(2,1)}), bf16[1024,512]{1,0:T(8,128)(2,1)}) %all-gather.19.cloned.1.call-update) | async-done | bytes 1048592 | tf_op jit(solution)/shard_map/all_gather | solution.py:42
  111.7 34.8 %all-gather.33.cloned.1.call-done = bf16[1,1024,512]{2,1,0:T(8,128)(2,1)} async-done(((bf16[1,128,512]{2,1,0:T(8,128)(2,1)}), bf16[1,1024,512]{2,1,0:T(8,128)(2,1)}) %all-gather.33.cloned.1.call-update) | async-done | bytes 1048592 | tf_op jit(solution)/shard_map/all_gather | solution.py:38
  151.7 35.8 %all-gather.35.cloned.1.call-done = bf16[1,1024,512]{2,1,0:T(8,128)(2,1)} async-done(((bf16[1,128,512]{2,1,0:T(8,128)(2,1)}), bf16[1,1024,512]{2,1,0:T(8,128)(2,1)}) %all-gather.35.cloned.1.call-update) | async-done | bytes 1048592 | tf_op jit(solution)/shard_map/all_gather | solution.py:37
  189.2 39.4 %all-gather.21.cloned.1.call-done = bf16[1024,512]{1,0:T(8,128)(2,1)} async-done(((bf16[128,512]{1,0:T(8,128)(2,1)}), bf16[1024,512]{1,0:T(8,128)(2,1)}) %all-gather.21.cloned.1.call-update) | async-done | bytes 1048592 | tf_op jit(solution)/shard_map/all_gather | solution.py:42
  232.6 37.0 %all-gather.23.cloned.1.call-done = bf16[1024,512]{1,0:T(8,128)(2,1)} async-done(((bf16[128,512]{1,0:T(8,128)(2,1)}), bf16[1024,512]{1,0:T(8,128)(2,1)}) %all-gather.23.cloned.1.call-update) | async-done | bytes 1048592 | tf_op jit(solution)/shard_map/all_gather | solution.py:42
  279.7 46.5 %collective-permute-done.15 = f32[4,128,1024]{2,1,0:T(8,128)} collective-permute-done((f32[4,128,1024]{2,1,0:T(8,128)}, f32[4,128,1024]{2,1,0:T(8,128)}, u32[]{:S(2)}, u32[]{:S(2)}) %collective-permute-start.15) | collective-permute-done | bytes 2097184 | tf_op jit(solution)/shard_map/ppermute | solution.py:18
  326.2 4.4 fusion.129
  332.4 39.1 %all-gather.37.cloned.1.call-done = bf16[1,1024,512]{2,1,0:T(8,128)(2,1)} async-done(((bf16[1,128,512]{2,1,0:T(8,128)(2,1)}), bf16[1,1024,512]{2,1,0:T(8,128)(2,1)}) %all-gather.37.cloned.1.call-update) | async-done | bytes 1048592 | tf_op jit(solution)/shard_map/all_gather | solution.py:36
  374.6 3.5 collective-permute-done.16
  380.5 37.6 %all-gather.25.cloned.1.call-done = bf16[1024,512]{1,0:T(8,128)(2,1)} async-done(((bf16[128,512]{1,0:T(8,128)(2,1)}), bf16[1024,512]{1,0:T(8,128)(2,1)}) %all-gather.25.cloned.1.call-update) | async-done | bytes 1048592 | tf_op jit(solution)/shard_map/all_gather | solution.py:42
  421.4 3.5 collective-permute-done.17
  427.2 4.7 collective-permute-done.18
  433.0 26.2 %all-gather.39.cloned.1.call-done = bf16[1,1024,512]{2,1,0:T(8,128)(2,1)} async-done(((bf16[1,128,512]{2,1,0:T(8,128)(2,1)}), bf16[1,1024,512]{2,1,0:T(8,128)(2,1)}) %all-gather.39.cloned.1.call-update) | async-done | bytes 1048592 | tf_op jit(solution)/shard_map/all_gather | solution.py:38
  462.3 3.5 collective-permute-done.20
  469.4 30.8 %all-gather.41.cloned.1.call-done = bf16[1,1024,512]{2,1,0:T(8,128)(2,1)} async-done(((bf16[1,128,512]{2,1,0:T(8,128)(2,1)}), bf16[1,1024,512]{2,1,0:T(8,128)(2,1)}) %all-gather.41.cloned.1.call-update) | async-done | bytes 1048592 | tf_op jit(solution)/shard_map/all_gather | solution.py:37
  503.2 38.1 %all-gather.27.cloned.1.call-done = bf16[1024,512]{1,0:T(8,128)(2,1)} async-done(((bf16[128,512]{1,0:T(8,128)(2,1)}), bf16[1024,512]{1,0:T(8,128)(2,1)}) %all-gather.27.cloned.1.call-update) | async-done | bytes 1048592 | tf_op jit(solution)/shard_map/all_gather | solution.py:42
  546.5 3.0 collective-permute-done.25
  550.3 32.0 %all-gather.29.cloned.1.call-done = bf16[1024,512]{1,0:T(8,128)(2,1)} async-done(((bf16[128,512]{1,0:T(8,128)(2,1)}), bf16[1024,512]{1,0:T(8,128)(2,1)}) %all-gather.29.cloned.1.call-update) | async-done | bytes 1048592 | tf_op jit(solution)/shard_map/all_gather | solution.py:42
  588.6 10.2 %collective-permute-done.22 = f32[128,512]{1,0:T(8,128)S(1)} collective-permute-done((f32[128,512]{1,0:T(8,128)S(1)}, f32[128,512]{1,0:T(8,128)S(1)}, u32[]{:S(2)}, u32[]{:S(2)}) %collective-permute-start.22) | collective-permute-done | bytes 262176 | tf_op jit(solution)/shard_map/ppermute | solution.py:18
  600.3 4.1 collective-permute-done.26
  (172 shorter events, 77.3 us)
Async XLA Ops:
  6.5 56.0 %all-gather.31.cloned.1.call-start = ((), (), s32[]{:S(2)}) async-start(), calls=%async_computation.6 | async-start | bytes 1179648 | tf_op jit(solution)/shard_map/all_gather | solution.py:36
  19.5 85.9 %all-gather.19.cloned.1.call-start = ((), (), s32[]{:S(2)}) async-start(), calls=%async_computation | async-start | bytes 1179648 | tf_op jit(solution)/shard_map/all_gather | solution.py:42
  66.2 80.3 %all-gather.33.cloned.1.call-start = ((), (), s32[]{:S(2)}) async-start(), calls=%async_computation.7 | async-start | bytes 1179648 | tf_op jit(solution)/shard_map/all_gather | solution.py:38
  67.0 120.6 %all-gather.35.cloned.1.call-start = ((), (), s32[]{:S(2)}) async-start(), calls=%async_computation.8 | async-start | bytes 1179648 | tf_op jit(solution)/shard_map/all_gather | solution.py:37
  67.8 160.8 %all-gather.21.cloned.1.call-start = ((), (), s32[]{:S(2)}) async-start(), calls=%async_computation.1 | async-start | bytes 1179648 | tf_op jit(solution)/shard_map/all_gather | solution.py:42
  111.7 157.9 %all-gather.23.cloned.1.call-start = ((), (), s32[]{:S(2)}) async-start(), calls=%async_computation.2 | async-start | bytes 1179648 | tf_op jit(solution)/shard_map/all_gather | solution.py:42
  150.4 221.2 %all-gather.37.cloned.1.call-start = ((), (), s32[]{:S(2)}) async-start(), calls=%async_computation.9 | async-start | bytes 1179648 | tf_op jit(solution)/shard_map/all_gather | solution.py:36
  150.7 36.8 %collective-permute-start.9 = (bf16[128,512]{1,0:T(8,128)(2,1)S(1)}, bf16[128,512]{1,0:T(8,128)(2,1)S(1)}, u32[]{:S(2)}, u32[]{:S(2)}) collective-permute-start(bf16[128,512]{1,0:T(8,128)(2,1)S(1)} %fusion.36), channel_id=1, source_target_pairs={{0,8},{8,0},{16,24},{24,16},{1,9},{9,1},{17,25},{25,17},{2,10},{10... | collective-permute-start | bytes 393224 | tf_op jit(solution)/shard_map/ppermute | solution.py:18
  151.3 122.5 %collective-permute-start.8 = (f32[128,512]{1,0:T(8,128)S(1)}, f32[128,512]{1,0:T(8,128)S(1)}, u32[]{:S(2)}, u32[]{:S(2)}) collective-permute-start(f32[128,512]{1,0:T(8,128)S(1)} %fusion.32), channel_id=1, source_target_pairs={{0,8},{8,0},{16,24},{24,16},{1,9},{9,1},{17,25},{25,17},{2,10},{10... | collective-permute-start | bytes 786440 | tf_op jit(solution)/shard_map/ppermute | solution.py:18
  189.1 86.4 %collective-permute-start.12 = (f32[128,512]{1,0:T(8,128)S(1)}, f32[128,512]{1,0:T(8,128)S(1)}, u32[]{:S(2)}, u32[]{:S(2)}) collective-permute-start(f32[128,512]{1,0:T(8,128)S(1)} %fusion.28), channel_id=1, source_target_pairs={{0,8},{8,0},{16,24},{24,16},{1,9},{9,1},{17,25},{25,17},{2,10},{10... | collective-permute-start | bytes 786440 | tf_op jit(solution)/shard_map/ppermute | solution.py:18
  231.6 38.0 %collective-permute-start.4 = (bf16[128,512]{1,0:T(8,128)(2,1)S(1)}, bf16[128,512]{1,0:T(8,128)(2,1)S(1)}, u32[]{:S(2)}, u32[]{:S(2)}) collective-permute-start(bf16[128,512]{1,0:T(8,128)(2,1)S(1)} %fusion.83), channel_id=1, source_target_pairs={{0,8},{8,0},{16,24},{24,16},{1,9},{9,1},{17,25},{25,17},{2,10},{10... | collective-permute-start | bytes 393224 | tf_op jit(solution)/shard_map/ppermute | solution.py:18
  232.5 40.0 %collective-permute-start.13 = (bf16[128,512]{1,0:T(8,128)(2,1)S(1)}, bf16[128,512]{1,0:T(8,128)(2,1)S(1)}, u32[]{:S(2)}, u32[]{:S(2)}) collective-permute-start(bf16[128,512]{1,0:T(8,128)(2,1)S(1)} %fusion.119), channel_id=1, source_target_pairs={{0,8},{8,0},{16,24},{24,16},{1,9},{9,1},{17,25},{25,17},{2,10},{10... | collective-permute-start | bytes 393224 | tf_op jit(solution)/shard_map/ppermute | solution.py:18
  278.3 48.0 %collective-permute-start.15 = (f32[4,128,1024]{2,1,0:T(8,128)}, f32[4,128,1024]{2,1,0:T(8,128)}, u32[]{:S(2)}, u32[]{:S(2)}) collective-permute-start(f32[4,128,1024]{2,1,0:T(8,128)} %pad_maximum_fusion), channel_id=1, source_target_pairs={{0,16},{16,0},{8,24},{24,8},{1,17},{17,1},{9,25},{25,9},{2,18},{18... | collective-permute-start | bytes 6291464 | tf_op jit(solution)/shard_map/ppermute | solution.py:18
  332.4 85.6 %all-gather.25.cloned.1.call-start = ((), (), s32[]{:S(2)}) async-start(), calls=%async_computation.3 | async-start | bytes 1179648 | tf_op jit(solution)/shard_map/all_gather | solution.py:42
  378.9 80.3 %all-gather.39.cloned.1.call-start = ((), (), s32[]{:S(2)}) async-start(), calls=%async_computation.10 | async-start | bytes 1179648 | tf_op jit(solution)/shard_map/all_gather | solution.py:38
  379.6 120.5 %all-gather.41.cloned.1.call-start = ((), (), s32[]{:S(2)}) async-start(), calls=%async_computation.11 | async-start | bytes 1179648 | tf_op jit(solution)/shard_map/all_gather | solution.py:37
  380.4 160.9 %all-gather.27.cloned.1.call-start = ((), (), s32[]{:S(2)}) async-start(), calls=%async_computation.4 | async-start | bytes 1179648 | tf_op jit(solution)/shard_map/all_gather | solution.py:42
  432.7 149.6 %all-gather.29.cloned.1.call-start = ((), (), s32[]{:S(2)}) async-start(), calls=%async_computation.5 | async-start | bytes 1179648 | tf_op jit(solution)/shard_map/all_gather | solution.py:42
  466.9 33.2 %collective-permute-start.24 = (bf16[128,512]{1,0:T(8,128)(2,1)S(1)}, bf16[128,512]{1,0:T(8,128)(2,1)S(1)}, u32[]{:S(2)}, u32[]{:S(2)}) collective-permute-start(bf16[128,512]{1,0:T(8,128)(2,1)S(1)} %fusion.22), channel_id=1, source_target_pairs={{0,16},{16,0},{8,24},{24,8},{1,17},{17,1},{9,25},{25,9},{2,18},{18... | collective-permute-start | bytes 393224 | tf_op jit(solution)/shard_map/ppermute | solution.py:18
  468.8 131.6 %collective-permute-start.23 = (f32[128,512]{1,0:T(8,128)S(1)}, f32[128,512]{1,0:T(8,128)S(1)}, u32[]{:S(2)}, u32[]{:S(2)}) collective-permute-start(f32[128,512]{1,0:T(8,128)S(1)} %fusion.18), channel_id=1, source_target_pairs={{0,16},{16,0},{8,24},{24,8},{1,17},{17,1},{9,25},{25,9},{2,18},{18... | collective-permute-start | bytes 786440 | tf_op jit(solution)/shard_map/ppermute | solution.py:18
  501.7 104.1 %collective-permute-start.27 = (f32[128,512]{1,0:T(8,128)S(1)}, f32[128,512]{1,0:T(8,128)S(1)}, u32[]{:S(2)}, u32[]{:S(2)}) collective-permute-start(f32[128,512]{1,0:T(8,128)S(1)} %fusion.14), channel_id=1, source_target_pairs={{0,16},{16,0},{8,24},{24,8},{1,17},{17,1},{9,25},{25,9},{2,18},{18... | collective-permute-start | bytes 786440 | tf_op jit(solution)/shard_map/ppermute | solution.py:18
  545.8 36.5 %collective-permute-start.19 = (bf16[128,512]{1,0:T(8,128)(2,1)S(1)}, bf16[128,512]{1,0:T(8,128)(2,1)S(1)}, u32[]{:S(2)}, u32[]{:S(2)}) collective-permute-start(bf16[128,512]{1,0:T(8,128)(2,1)S(1)} %fusion.82), channel_id=1, source_target_pairs={{0,16},{16,0},{8,24},{24,8},{1,17},{17,1},{9,25},{25,9},{2,18},{18... | collective-permute-start | bytes 393224 | tf_op jit(solution)/shard_map/ppermute | solution.py:18
  549.8 37.0 %collective-permute-start.28 = (bf16[128,512]{1,0:T(8,128)(2,1)S(1)}, bf16[128,512]{1,0:T(8,128)(2,1)S(1)}, u32[]{:S(2)}, u32[]{:S(2)}) collective-permute-start(bf16[128,512]{1,0:T(8,128)(2,1)S(1)} %fusion.109), channel_id=1, source_target_pairs={{0,16},{16,0},{8,24},{24,8},{1,17},{17,1},{9,25},{25,9},{2,18},{18... | collective-permute-start | bytes 393224 | tf_op jit(solution)/shard_map/ppermute | solution.py:18
  583.9 20.7 %collective-permute-start.21 = (f32[128,512]{1,0:T(8,128)S(1)}, f32[128,512]{1,0:T(8,128)S(1)}, u32[]{:S(2)}, u32[]{:S(2)}) collective-permute-start(f32[128,512]{1,0:T(8,128)S(1)} %fusion.117), channel_id=1, source_target_pairs={{0,16},{16,0},{8,24},{24,8},{1,17},{17,1},{9,25},{25,9},{2,18},{18... | collective-permute-start | bytes 786440 | tf_op jit(solution)/shard_map/ppermute | solution.py:18
  (35 other events, 300.3 us)
Sparse Core Ops, SparseCore 0:
  19.6 42.8 all-gather.30
  66.4 38.9 all-gather.18
  107.5 38.9 all-gather.32
  148.5 38.9 all-gather.34
  189.5 38.9 all-gather.20
  230.5 39.0 all-gather.22
  332.5 38.9 all-gather.36
  379.0 38.9 all-gather.24
  420.2 38.9 all-gather.38
  461.1 38.9 all-gather.40
  502.3 38.9 all-gather.26
  543.3 38.9 all-gather.28
where the time goes:
time: 618 us; the launch traced here: 617 us
  waiting for transfers between devices  522 us (84%)
  matrix products  29.3 us (5%)
  starting transfers between devices  23.3 us (4%)
  other arithmetic  20.7 us (3%)
  between operations  14.1 us (2%)
  local copies, waits for them, and re-layouts  7.5 us (1%)
    all_gather x6, waiting for transfers between devices, spread(): return lax.all_gather(cut_cols(values), 'panel', axis=0, tiled=True)  222 us
    ppermute x30, waiting for transfers between devices, partner_2(): return lax.ppermute(block, axis, route)  90.4 us
    all_gather x2, waiting for transfers between devices, star(): lax.all_gather(cut_cols(head_bottom), 'panel', axis=0, tiled=True)  82.1 us
    all_gather x2, waiting for transfers between devices, star(): lax.all_gather(cut_cols(tail_up), 'panel', axis=0, tiled=True)  66.6 us
    all_gather x2, waiting for transfers between devices, star(): lax.all_gather(cut_cols(head_down), 'panel', axis=0, tiled=True)  61 us
    dot_general x28, matrix products, multiply(): jnp.dot(to_half(left), right, preferred_element_type=jnp.float32)  27 us
    ppermute x30, starting transfers between devices, partner_2(): return lax.ppermute(block, axis, route)  22.7 us
  transfers between devices with their start and end apart: 42, of which 28 were waited for; matrix products, arithmetic and copies ran while one was open for 5% of the time, Pallas kernels for 0%

commit v1 on v0

v1 whole, which is shorter than its diff:
```python
import functools
import jax
import jax.numpy as jnp
from jax import lax
from jax.experimental import pallas as pl
from jax.experimental.pallas import tpu as pltpu
from jax.sharding import PartitionSpec as P

BLK = 64
TILE = 256
MESH = pl.DeviceIdType.MESH


def kernel(outer, inner, counts, first_ref, second_ref, left_ref, add_ref, own_ref, other_ref,
           right, swap, base, front, mid, recv_sem, send_sem, swap_recv, swap_send, local_sem, last_recv, last_send):
    rows, width = left_ref.shape
    slab = lax.axis_index("slab")
    panel = lax.axis_index("panel")
    core = slab % 2
    side = (slab // 2) % 2
    sibling = slab + 1 - 2 * core
    partner = slab + 2 - 4 * side
    out_pos = panel // inner
    in_pos = panel % inner

    def flip(value, bits):
        result = value
        for bit in range(6):
            if bits >> bit & 1:
                result = result + (1 << bit) * (1 - 2 * ((value // (1 << bit)) % 2))
        return result

    outer_peers = [flip(out_pos, i) * inner + in_pos for i in range(1, outer)]
    inner_bits = range(1, inner)

    barrier = pltpu.get_barrier_semaphore()
    friends = [(slab, p) for p in outer_peers]
    friends += [(slab, out_pos * inner + flip(in_pos, j)) for j in inner_bits]
    friends += [(sibling, panel), (partner, panel)]
    for friend in friends:
        pl.semaphore_signal(barrier, inc=1, device_id=friend, device_id_type=MESH)
    pl.semaphore_wait(barrier, len(friends))

    sent = []
    used = [0]

    def place(level, kind, owner, p):
        return right.at[level, kind, owner, pl.ds(pl.multiple_of(p * rows, rows), rows), :]

    def push(level, kind, src, p, target):
        spot = used[0]
        used[0] += 1
        copy = pltpu.make_async_remote_copy(
            src_ref=src, dst_ref=place(level, kind, core, p), send_sem=send_sem.at[spot],
            recv_sem=recv_sem.at[level, kind, core, p], device_id=target, device_id_type=MESH)
        copy.start()
        sent.append(copy)

    def arrive(level, kind, owner, p):
        spot = place(level, kind, owner, p)
        pltpu.make_async_remote_copy(
            src_ref=spot, dst_ref=spot, send_sem=send_sem.at[0],
            recv_sem=recv_sem.at[level, kind, owner, p], device_id=(sibling, panel), device_id_type=MESH).wait_recv()

    def to_inner(level, kind, src, p):
        for j in inner_bits:
            push(level, kind, src, p, (slab, out_pos * inner + flip(in_pos, j)))

    def to_sibling(level, kind, src, p):
        push(level, kind, src, p, (sibling, panel))

    def open_gather(level, kind, src):
        copy = pltpu.make_async_copy(src, place(level, kind, core, panel), local_sem.at[level, kind])
        copy.start()
        for p in outer_peers:
            push(level, kind, src, panel, (slab, p))
        to_inner(level, kind, src, panel)
        to_sibling(level, kind, src, panel)
        return copy

    def relay_outer(level, kind, i):
        p = outer_peers[i]
        arrive(level, kind, core, p)
        to_inner(level, kind, place(level, kind, core, p), p)
        to_sibling(level, kind, place(level, kind, core, p), p)

    def relay_inner(level, kind):
        for i in range(outer):
            for j in inner_bits:
                p = flip(out_pos, i) * inner + flip(in_pos, j)
                arrive(level, kind, core, p)
                to_sibling(level, kind, place(level, kind, core, p), p)

    def settle(level, kind, copy):
        for i in range(outer):
            for j in range(inner):
                arrive(level, kind, 1 - core, flip(out_pos, i) * inner + flip(in_pos, j))
        copy.wait()

    def product(left, factor, emit):
        @pl.loop(0, width // TILE)
        def _(step):
            cols = pl.ds(pl.multiple_of(step * TILE, TILE), TILE)
            emit(cols, jnp.dot(left[...], factor[:, cols], preferred_element_type=jnp.float32))

    def keep(ref):
        def emit(cols, value):
            ref[:, cols] = value.astype(ref.dtype)
        return emit

    def keep_sum(ref, extra):
        def emit(cols, value):
            ref[:, cols] = (extra[:, cols].astype(jnp.float32) + value).astype(ref.dtype)
        return emit

    is_tail = core == 1

    def merge(level, first, second, left, add, outs, after_diag):
        copies = [open_gather(level, 0, first), open_gather(level, 1, second())]
        for i in range(outer - 1):
            relay_outer(level, 0, i)
        relay_inner(level, 0)
        settle(level, 0, copies[0])
        top = right.at[level, 0, 1 - level]
        bottom = right.at[level, 0, level]

        @pl.when(is_tail)
        def _():
            product(left, bottom, keep(base))

        @pl.when(core == 0)
        def _():
            base[...] = left[...]

        pending = list(range(outer - 1))
        for turn in range(3):
            product(base if turn == 0 else front, top, keep(mid))
            if pending:
                relay_outer(level, 1, pending.pop(0))
            product(mid, bottom, keep_sum(front, base))
        for i in pending:
            relay_outer(level, 1, i)
        product(front, top, keep(mid))
        relay_inner(level, 1)

        @pl.when(is_tail)
        def _():
            front[...] = (left[...].astype(jnp.float32) + mid[...].astype(jnp.float32)).astype(front.dtype)
            product(mid, bottom, keep_sum(base, base))

        @pl.when(core == 0)
        def _():
            base[...] = mid[...]

        settle(level, 1, copies[1])
        mine = right.at[level, 1, core]
        theirs = right.at[level, 1, 1 - core]
        diag_factor, side_factor = (mine, theirs) if level == 0 else (theirs, mine)
        product(base, diag_factor, keep_sum(outs[0], add))
        after_diag()
        product(front, side_factor, keep(outs[1]))

    gives = lax.rem(side + core, 2)
    slot = 1 - gives

    def swap_copy(kind, which):
        return pltpu.make_async_remote_copy(
            src_ref=swap.at[which, kind], dst_ref=swap.at[which, kind], send_sem=swap_send.at[kind],
            recv_sem=swap_recv.at[kind], device_id=(partner, panel), device_id_type=MESH)

    merge(0, first_ref, lambda: second_ref, left_ref, add_ref,
          (swap.at[slot, 0], swap.at[slot, 1]), lambda: swap_copy(0, slot).start())
    swap_copy(1, slot).start()
    swap_copy(0, gives).wait_recv()

    def swap_second():
        swap_copy(1, gives).wait_recv()
        return swap.at[0, 1]

    def last_copy(kind):
        return pltpu.make_async_remote_copy(
            src_ref=own_ref.at[kind], dst_ref=other_ref.at[kind], send_sem=last_send.at[kind],
            recv_sem=last_recv.at[kind], device_id=(sibling, panel), device_id_type=MESH)

    merge(1, swap.at[0, 0], swap_second, swap.at[1, 1], swap.at[1, 0],
          (own_ref.at[0], own_ref.at[1]), lambda: last_copy(0).start())
    last_copy(1).start()
    for kind in range(2):
        swap_copy(kind, slot).wait_send()
    for copy in sent:
        copy.wait_send()
    for kind in range(2):
        last_copy(kind).wait()
    assert used[0] == counts


def body(panels, ranges, pattern):
    blocks = ranges[0]
    rows, width = blocks.shape[1:]
    count = pattern.shape[2]
    core = lax.axis_index("slab") % 2
    row_start = lax.axis_index("panel") * rows
    row_ids = row_start + jnp.arange(rows, dtype=jnp.int32)
    col_ids = jnp.arange(width, dtype=jnp.int32)
    block_ids = jnp.arange(count, dtype=jnp.int32)
    row_pick = (row_ids[:, None] // BLK == block_ids[None, :]).astype(jnp.float32)
    col_pick = (block_ids[:, None] == col_ids[None, :] // BLK).astype(jnp.float32)
    mask = jnp.einsum("mi,gij,jc->gmc", row_pick, pattern[0].astype(jnp.float32), col_pick)
    masked = blocks * mask
    half = masked.astype(jnp.bfloat16)
    head = core == 0
    first = jnp.where(head, half[3], half[0])
    second = jnp.where(head, half[2], half[1])
    left = jnp.where(head, half[1], half[2])
    add = jnp.where(head, masked[0], masked[3])

    outer = min(4, panels)
    inner = panels // outer
    counts = 4 * ((outer - 1) + (inner - 1) + 1 + (outer - 1) * inner + outer * (inner - 1))
    vmem = pl.BlockSpec(memory_space=pltpu.VMEM)
    own, other = pl.pallas_call(
        functools.partial(kernel, outer, inner, counts),
        out_shape=[jax.ShapeDtypeStruct((2, rows, width), jnp.float32)] * 2,
        in_specs=[vmem] * 4,
        out_specs=[vmem] * 2,
        scratch_shapes=[
            pltpu.VMEM((2, 2, 2, width, width), jnp.bfloat16),
            pltpu.VMEM((2, 2, rows, width), jnp.bfloat16),
            pltpu.VMEM((rows, width), jnp.bfloat16),
            pltpu.VMEM((rows, width), jnp.bfloat16),
            pltpu.VMEM((rows, width), jnp.bfloat16),
            pltpu.SemaphoreType.DMA((2, 2, 2, panels)),
            pltpu.SemaphoreType.DMA((counts,)),
            pltpu.SemaphoreType.DMA((2,)),
            pltpu.SemaphoreType.DMA((2,)),
            pltpu.SemaphoreType.DMA((2, 2)),
            pltpu.SemaphoreType.DMA((2,)),
            pltpu.SemaphoreType.DMA((2,)),
        ],
        compiler_params=pltpu.CompilerParams(
            collective_id=0, has_side_effects=True, vmem_limit_bytes=48 << 20),
        name="merge_levels",
    )(first, second, left, add)
    return jnp.stack([
        jnp.where(head, own[0], other[0]),
        jnp.where(head, own[1], other[1]),
        jnp.where(head, other[1], own[1]),
        jnp.where(head, other[0], own[0]),
    ])[None]


def solution(mesh):
    return jax.shard_map(
        functools.partial(body, mesh.shape["panel"]),
        mesh=mesh,
        in_specs=(P("slab", None, "panel", None), P("slab", None, None, None)),
        out_specs=P("slab", None, "panel", None),
        check_vma=False,
    )
```

time: 618 us -> 147 us (0.24)
  the two profiles are of different devices: /device:TPU:0 before, /device:TPU:9 now
where the time goes in v1:
time: 147 us; the launch traced here: 146 us
  Pallas kernels  142 us (97%)
  matrix products  2.31 us (2%)
  other arithmetic  1.76 us (1%)
    pallas_call x1, Pallas kernels, body(): pl.pallas_call(functools.partial(kernel, outer, inner, counts), out_shape...  142 us

profile of v1, /device:TPU:9, one launch (start us, length us, event | category | flops | bytes accessed | tf_op | source)
XLA Modules:
  0.0 146.5 jit_solution(8227424024065729297)
XLA Ops:
  0.0 2.3 %fusion.17 = (bf16[4,128,1024]{2,1,0:T(8,128)(2,1)S(1)}, f32[4,128,1024]{2,1,0:T(8,128)S(1)}) fusion(s32[1024]{0:T(1024)S(1)} %add_select_fusion, s32[1,4,16,16]{3,2,1,0:T(8,128)} %param.3, s32[128]{0:T(128)S(1)} %and_select_fusion, f32[1,4,128,1024]{3,2,1,0:T(8,128)} %param.2), kind=kOutput, calls=%fused_computation.32 | convolution fusion | flops 18107392 | bytes 5251584 | tf_op jit(solution)/shard_map/mi,gij,jc->gmc/dot_general | solution.py:208
  2.3 0.1 select_bitcast_fusion
  2.4 0.1 fusion.add_ref
  2.5 142.4 %merge_levels.1 = (f32[2,128,1024]{2,1,0:T(8,128)S(1)}, f32[2,128,1024]{2,1,0:T(8,128)S(1)}) custom-call(bf16[128,1024]{1,0:T(8,128)(2,1)S(1)} %get-tuple-element.15.first_ref, bf16[128,1024]{1,0:T(8,128)(2,1)S(1)} %get-tuple-element.14.second_ref, bf16[128,1024]{1,0:T(8,128)(2,1)S(1)} %get-tuple-element.13.left_ref, f32[128,1024]{1,0:T(8,128)S(1)} %fusion.add_ref), custom_call_target="tpu_custom_call" | custom-call | tf_op jit(solution)/shard_map/merge_levels/pallas_call | solution.py:221
  144.8 0.2 slice_select_fusion.4
  145.0 1.5 maximum_bitcast_fusion
  (2 shorter events, 0.0 us)

commit v2 on v1

v2 whole, which is shorter than its diff:
```python
import functools
import jax
import jax.numpy as jnp
from jax import lax
from jax.experimental import pallas as pl
from jax.experimental.pallas import tpu as pltpu
from jax.sharding import PartitionSpec as P

BLK = 64
TILE = 256
MESH = pl.DeviceIdType.MESH


def kernel(outer, inner, counts, first_ref, second_ref, left_ref, add_ref, own_ref, other_ref,
           right, swap, base, front, mid, recv_sem, send_sem, swap_recv, swap_send, local_sem, last_recv, last_send):
    rows, width = left_ref.shape
    panels = outer * inner
    slab = lax.axis_index("slab")
    panel = lax.axis_index("panel")
    core = slab % 2
    side = (slab // 2) % 2
    sibling = slab + 1 - 2 * core
    partner = slab + 2 - 4 * side
    out_pos = panel // inner
    in_pos = panel % inner

    column = panel % inner
    rise = panel // inner
    spot_here = column * outer + rise + (outer - 1 - 2 * rise) * (column % 2)

    def at_ring(shift):
        where = (spot_here + shift + panels) % panels
        turn = where // outer
        step = where % outer
        return (step + (outer - 1 - 2 * step) * (turn % 2)) * inner + turn

    ahead = (slab, at_ring(1))
    behind = (slab, at_ring(-1))

    barrier = pltpu.get_barrier_semaphore()
    friends = [ahead, behind, (sibling, panel), (partner, panel)]
    for friend in friends:
        pl.semaphore_signal(barrier, inc=1, device_id=friend, device_id_type=MESH)
    pl.semaphore_wait(barrier, len(friends))

    sent = []
    piece = rows // 2
    reach = panels // 2

    def place(level, kind, owner, p, half):
        return right.at[level, kind, owner, pl.ds(pl.multiple_of(p * rows + half * piece, piece), piece), :]

    def push(level, kind, src, p, half, target, guard):
        spot = len(sent)
        sent.append(guard)
        pltpu.make_async_remote_copy(
            src_ref=src, dst_ref=place(level, kind, core, p, half), send_sem=send_sem.at[spot],
            recv_sem=recv_sem.at[level, kind, core, p, half], device_id=target, device_id_type=MESH).start()

    def arrive(level, kind, owner, p, half):
        spot = place(level, kind, owner, p, half)
        pltpu.make_async_remote_copy(
            src_ref=spot, dst_ref=spot, send_sem=send_sem.at[0], recv_sem=recv_sem.at[level, kind, owner, p, half],
            device_id=(sibling, panel), device_id_type=MESH).wait_recv()

    def share(level, kind, src, p, half, guard):
        if guard == "gives":
            push(level, kind, src, p, half, (partner, panel), guard)
        push(level, kind, src, p, half, (sibling, panel), guard)

    def local_copy(level, kind, src):
        return pltpu.make_async_copy(src, right.at[level, kind, core, pl.ds(pl.multiple_of(panel * rows, rows), rows), :],
                                     local_sem.at[level, kind])

    def open_ring(level, kind, src, guard=None):
        local_copy(level, kind, src).start()
        parts = [src.at[pl.ds(half * piece, piece), :] for half in range(2)]
        for half in range(2):
            push(level, kind, parts[half], panel, half, ahead, guard)
            push(level, kind, parts[half], panel, half, behind, guard)
        for half in range(2):
            share(level, kind, parts[half], panel, half, guard)

    def items(distance):
        for half in range(2):
            for way in (1, -1):
                if distance < reach or (half == 0) == (way == 1):
                    passes = distance + 1 < reach or (distance + 1 == reach and (half == 0) == (way == 1))
                    yield half, way, passes

    def relay(level, kind, distance, guard=None):
        for half, way, passes in items(distance):
            p = at_ring(-way * distance)
            arrive(level, kind, core, p, half)
            src = place(level, kind, core, p, half)
            if passes:
                push(level, kind, src, p, half, ahead if way == 1 else behind, guard)
            share(level, kind, src, p, half, guard)

    def follow(level, kind, distance):
        pairs = [(half, way) for half, way, _ in items(distance)] if distance else [(0, 1), (1, 1)]
        for half, way in pairs:
            p = at_ring(-way * distance)
            arrive(level, kind, core, p, half)
            share(level, kind, place(level, kind, core, p, half), p, half, "takes")

    def settle(level, kind, src, guard=None):
        for distance in range(reach + 1):
            pairs = [(half, way) for half, way, _ in items(distance)] if distance else [(0, 1), (1, 1)]
            for half, way in pairs:
                arrive(level, kind, 1 - core, at_ring(-way * distance), half)
        if guard is None:
            local_copy(level, kind, src).wait()
        else:
            @pl.when(gives == 1)
            def _():
                local_copy(level, kind, src).wait()

    gives = (side + core) % 2
    slot = 1 - gives

    def product(left, factor, emit):
        @pl.loop(0, width // TILE)
        def _(step):
            cols = pl.ds(pl.multiple_of(step * TILE, TILE), TILE)
            emit(cols, jnp.dot(left[...], factor[:, cols], preferred_element_type=jnp.float32))

    def keep(ref):
        def emit(cols, value):
            ref[:, cols] = value.astype(ref.dtype)
        return emit

    def keep_sum(ref, extra):
        def emit(cols, value):
            ref[:, cols] = (extra[:, cols].astype(jnp.float32) + value).astype(ref.dtype)
        return emit

    def swap_copy(kind, which):
        return pltpu.make_async_remote_copy(
            src_ref=swap.at[which, kind], dst_ref=swap.at[which, kind], send_sem=swap_send.at[kind],
            recv_sem=swap_recv.at[kind], device_id=(partner, panel), device_id_type=MESH)

    is_tail = core == 1

    def merge(level, first, second, left, add, outs, after_diag):
        def run(action):
            if level == 0:
                action(None)
            else:
                pl.when(gives == 1)(lambda: action("gives"))

        def step(distance):
            run(lambda guard: relay(level, 1, distance, guard))
            if level == 1:
                pl.when(gives == 0)(lambda: follow(level, 1, distance))

        open_ring(level, 0, first)
        for distance in range(1, reach):
            relay(level, 0, distance)
        run(lambda guard: open_ring(level, 1, second, guard))
        relay(level, 0, reach)
        settle(level, 0, first)
        if level == 1:
            pl.when(gives == 0)(lambda: follow(level, 1, 0))
            pl.when(gives == 1)(lambda: swap_copy(1, 1).wait_recv())
        top = right.at[level, 0, 1 - level]
        bottom = right.at[level, 0, level]

        @pl.when(is_tail)
        def _():
            product(left, bottom, keep(base))

        @pl.when(core == 0)
        def _():
            base[...] = left[...]

        pending = list(range(1, reach + 1))
        early = max(len(pending) // 4, 1)

        def some():
            for _ in range(early):
                if pending:
                    step(pending.pop(0))

        for turn in range(3):
            product(base if turn == 0 else front, top, keep(mid))
            some()
            product(mid, bottom, keep_sum(front, base))
        product(front, top, keep(mid))

        @pl.when(is_tail)
        def _():
            front[...] = (left[...].astype(jnp.float32) + mid[...].astype(jnp.float32)).astype(front.dtype)
            product(mid, bottom, keep_sum(base, base))

        @pl.when(core == 0)
        def _():
            base[...] = mid[...]

        while pending:
            step(pending.pop(0))
        settle(level, 1, second, None if level == 0 else "gives")
        mine = right.at[level, 1, core]
        theirs = right.at[level, 1, 1 - core]
        diag_factor, side_factor = (mine, theirs) if level == 0 else (theirs, mine)
        product(base, diag_factor, keep_sum(outs[0], add))
        after_diag()
        product(front, side_factor, keep(outs[1]))

    merge(0, first_ref, second_ref, left_ref, add_ref,
          (swap.at[slot, 0], swap.at[slot, 1]), lambda: swap_copy(0, slot).start())
    pl.when(gives == 0)(lambda: swap_copy(1, 1).start())
    swap_copy(0, gives).wait_recv()

    def last_copy(kind):
        return pltpu.make_async_remote_copy(
            src_ref=own_ref.at[kind], dst_ref=other_ref.at[kind], send_sem=last_send.at[kind],
            recv_sem=last_recv.at[kind], device_id=(sibling, panel), device_id_type=MESH)

    merge(1, swap.at[0, 0], swap.at[0, 1], swap.at[1, 1], swap.at[1, 0],
          (own_ref.at[0], own_ref.at[1]), lambda: last_copy(0).start())
    last_copy(1).start()
    swap_copy(0, slot).wait_send()
    pl.when(gives == 0)(lambda: swap_copy(1, 1).wait_send())

    def drain(guard):
        own = right.at[0, 0, 0, pl.ds(0, piece), :]
        for spot, kept in enumerate(sent):
            if kept == guard:
                pltpu.make_async_remote_copy(
                    src_ref=own, dst_ref=own, send_sem=send_sem.at[spot], recv_sem=recv_sem.at[0, 0, 0, 0, 0],
                    device_id=(sibling, panel), device_id_type=MESH).wait_send()

    drain(None)
    pl.when(gives == 1)(lambda: drain("gives"))
    pl.when(gives == 0)(lambda: drain("takes"))
    for kind in range(2):
        last_copy(kind).wait()
    assert len(sent) <= counts, len(sent)


def body(panels, ranges, pattern):
    blocks = ranges[0]
    rows, width = blocks.shape[1:]
    count = pattern.shape[2]
    core = lax.axis_index("slab") % 2
    row_start = lax.axis_index("panel") * rows
    row_ids = row_start + jnp.arange(rows, dtype=jnp.int32)
    col_ids = jnp.arange(width, dtype=jnp.int32)
    block_ids = jnp.arange(count, dtype=jnp.int32)
    row_pick = (row_ids[:, None] // BLK == block_ids[None, :]).astype(jnp.float32)
    col_pick = (block_ids[:, None] == col_ids[None, :] // BLK).astype(jnp.float32)
    mask = jnp.einsum("mi,gij,jc->gmc", row_pick, pattern[0].astype(jnp.float32), col_pick)
    masked = blocks * mask
    half = masked.astype(jnp.bfloat16)
    head = core == 0
    first = jnp.where(head, half[3], half[0])
    second = jnp.where(head, half[2], half[1])
    left = jnp.where(head, half[1], half[2])
    add = jnp.where(head, masked[0], masked[3])

    outer = min(4, panels)
    inner = panels // outer
    counts = 20 * panels
    vmem = pl.BlockSpec(memory_space=pltpu.VMEM)
    own, other = pl.pallas_call(
        functools.partial(kernel, outer, inner, counts),
        out_shape=[jax.ShapeDtypeStruct((2, rows, width), jnp.float32)] * 2,
        in_specs=[vmem] * 4,
        out_specs=[vmem] * 2,
        scratch_shapes=[
            pltpu.VMEM((2, 2, 2, width, width), jnp.bfloat16),
            pltpu.VMEM((2, 2, rows, width), jnp.bfloat16),
            pltpu.VMEM((rows, width), jnp.bfloat16),
            pltpu.VMEM((rows, width), jnp.bfloat16),
            pltpu.VMEM((rows, width), jnp.bfloat16),
            pltpu.SemaphoreType.DMA((2, 2, 2, panels, 2)),
            pltpu.SemaphoreType.DMA((counts,)),
            pltpu.SemaphoreType.DMA((2,)),
            pltpu.SemaphoreType.DMA((2,)),
            pltpu.SemaphoreType.DMA((2, 2)),
            pltpu.SemaphoreType.DMA((2,)),
            pltpu.SemaphoreType.DMA((2,)),
        ],
        compiler_params=pltpu.CompilerParams(
            collective_id=0, has_side_effects=True, vmem_limit_bytes=48 << 20),
        name="merge_levels",
    )(first, second, left, add)
    return jnp.stack([
        jnp.where(head, own[0], other[0]),
        jnp.where(head, own[1], other[1]),
        jnp.where(head, other[1], own[1]),
        jnp.where(head, other[0], own[0]),
    ])[None]


def solution(mesh):
    return jax.shard_map(
        functools.partial(body, mesh.shape["panel"]),
        mesh=mesh,
        in_specs=(P("slab", None, "panel", None), P("slab", None, None, None)),
        out_specs=P("slab", None, "panel", None),
        check_vma=False,
    )
```

time: 147 us -> 120 us (0.82)
  the two profiles are of different devices: /device:TPU:9 before, /device:TPU:0 now
where the time goes in v2:
time: 120 us; the launch traced here: 118 us
  Pallas kernels  114 us (95%)
  matrix products  2.3 us (2%)
  other arithmetic  1.76 us (1%)
    pallas_call x1, Pallas kernels, body(): pl.pallas_call(functools.partial(kernel, outer, inner, counts), out_shape...  114 us

profile of v2, /device:TPU:0, one launch (start us, length us, event | category | flops | bytes accessed | tf_op | source)
XLA Modules:
  0.0 118.1 jit_solution(10334480538661605091)
XLA Ops:
  0.0 2.3 %fusion.17 = (bf16[4,128,1024]{2,1,0:T(8,128)(2,1)S(1)}, f32[4,128,1024]{2,1,0:T(8,128)S(1)}) fusion(s32[1024]{0:T(1024)S(1)} %add_select_fusion, s32[1,4,16,16]{3,2,1,0:T(8,128)} %param.3, s32[128]{0:T(128)S(1)} %and_select_fusion, f32[1,4,128,1024]{3,2,1,0:T(8,128)} %param.2), kind=kOutput, calls=%fused_computation.32 | convolution fusion | flops 18107392 | bytes 5251584 | tf_op jit(solution)/shard_map/mi,gij,jc->gmc/dot_general | solution.py:253
  2.3 0.1 select_bitcast_fusion
  2.4 0.1 fusion.add_ref
  2.5 114.0 %merge_levels.1 = (f32[2,128,1024]{2,1,0:T(8,128)S(1)}, f32[2,128,1024]{2,1,0:T(8,128)S(1)}) custom-call(bf16[128,1024]{1,0:T(8,128)(2,1)S(1)} %get-tuple-element.15.first_ref, bf16[128,1024]{1,0:T(8,128)(2,1)S(1)} %get-tuple-element.14.second_ref, bf16[128,1024]{1,0:T(8,128)(2,1)S(1)} %get-tuple-element.13.left_ref, f32[128,1024]{1,0:T(8,128)S(1)} %fusion.add_ref), custom_call_target="tpu_custom_call" | custom-call | tf_op jit(solution)/shard_map/merge_levels/pallas_call | solution.py:266
  116.5 0.2 slice_select_fusion.4
  116.7 1.5 %maximum_bitcast_fusion = f32[1,4,128,1024]{3,2,1,0:T(8,128)} fusion(f32[1,128,1024]{2,1,0:T(8,128)S(1)} %get-tuple-element.10, f32[1,128,1024]{2,1,0:T(8,128)S(1)} %get-tuple-element.11, f32[1,128,1024]{2,1,0:T(8,128)S(1)} %get-tuple-element.12, f32[1,128,1024]{2,1,0:T(8,128)S(1)} %get-tuple-element.9), kind=kLoop, calls=%fused_computation | loop fusion | flops 1572864 | bytes 4194304 | tf_op jit(solution)/shard_map/broadcast_in_dim | solution.py:289
  (2 shorter events, 0.0 us)

commit v3 on v2

--- a/solution.py
+++ b/solution.py
@@ -12,7 +12,7 @@
 
 
 def kernel(outer, inner, counts, first_ref, second_ref, left_ref, add_ref, own_ref, other_ref,
-           right, swap, base, front, mid, recv_sem, send_sem, swap_recv, swap_send, local_sem, last_recv, last_send):
+           right, swap, sums, base, front, mid, recv_sem, send_sem, swap_recv, swap_send, local_sem, last_recv, last_send):
     rows, width = left_ref.shape
     panels = outer * inner
     slab = lax.axis_index("slab")
@@ -64,7 +64,7 @@
             device_id=(sibling, panel), device_id_type=MESH).wait_recv()
 
     def share(level, kind, src, p, half, guard):
-        if guard == "gives":
+        if guard == "gives" and kind == 1:
             push(level, kind, src, p, half, (partner, panel), guard)
         push(level, kind, src, p, half, (sibling, panel), guard)
 
@@ -72,14 +72,15 @@
         return pltpu.make_async_copy(src, right.at[level, kind, core, pl.ds(pl.multiple_of(panel * rows, rows), rows), :],
                                      local_sem.at[level, kind])
 
-    def open_ring(level, kind, src, guard=None):
+    def open_ring(level, kind, src, guard=None, ready=None):
+        for half in range(2):
+            if ready:
+                ready(half)
+            part = src.at[pl.ds(half * piece, piece), :]
+            push(level, kind, part, panel, half, ahead, guard)
+            push(level, kind, part, panel, half, behind, guard)
+            share(level, kind, part, panel, half, guard)
         local_copy(level, kind, src).start()
-        parts = [src.at[pl.ds(half * piece, piece), :] for half in range(2)]
-        for half in range(2):
-            push(level, kind, parts[half], panel, half, ahead, guard)
-            push(level, kind, parts[half], panel, half, behind, guard)
-        for half in range(2):
-            share(level, kind, parts[half], panel, half, guard)
 
     def items(distance):
         for half in range(2):
@@ -104,17 +105,11 @@
             arrive(level, kind, core, p, half)
             share(level, kind, place(level, kind, core, p, half), p, half, "takes")
 
-    def settle(level, kind, src, guard=None):
-        for distance in range(reach + 1):
+    def settle(level, kind, distances):
+        for distance in distances:
             pairs = [(half, way) for half, way, _ in items(distance)] if distance else [(0, 1), (1, 1)]
             for half, way in pairs:
                 arrive(level, kind, 1 - core, at_ring(-way * distance), half)
-        if guard is None:
-            local_copy(level, kind, src).wait()
-        else:
-            @pl.when(gives == 1)
-            def _():
-                local_copy(level, kind, src).wait()
 
     gives = (side + core) % 2
     slot = 1 - gives
@@ -135,14 +130,15 @@
             ref[:, cols] = (extra[:, cols].astype(jnp.float32) + value).astype(ref.dtype)
         return emit
 
-    def swap_copy(kind, which):
+    def swap_copy(which):
+        ref = swap.at[0, 0, pl.ds(which * piece, piece), :] if which < 2 else swap.at[1, 3 - which]
         return pltpu.make_async_remote_copy(
-            src_ref=swap.at[which, kind], dst_ref=swap.at[which, kind], send_sem=swap_send.at[kind],
-            recv_sem=swap_recv.at[kind], device_id=(partner, panel), device_id_type=MESH)
+            src_ref=ref, dst_ref=ref, send_sem=swap_send.at[which],
+            recv_sem=swap_recv.at[which], device_id=(partner, panel), device_id_type=MESH)
 
     is_tail = core == 1
 
-    def merge(level, first, second, left, add, outs, after_diag):
+    def merge(level, lead, first, second, left, add, outs, after_diag):
         def run(action):
             if level == 0:
                 action(None)
@@ -154,15 +150,22 @@
             if level == 1:
                 pl.when(gives == 0)(lambda: follow(level, 1, distance))
 
-        open_ring(level, 0, first)
+        split = rows % 128 == 0
+        if level == 0:
+            open_ring(level, 0, first)
         for distance in range(1, reach):
             relay(level, 0, distance)
-        run(lambda guard: open_ring(level, 1, second, guard))
+            if distance == lead:
+                run(lambda guard: open_ring(level, 1, second, guard))
+                if level == 1:
+                    pl.when(gives == 0)(lambda: follow(level, 1, 0))
+            if distance > lead:
+                step(distance - lead)
         relay(level, 0, reach)
-        settle(level, 0, first)
+        settle(level, 0, range(reach + 1))
+        local_copy(level, 0, first).wait()
         if level == 1:
-            pl.when(gives == 0)(lambda: follow(level, 1, 0))
-            pl.when(gives == 1)(lambda: swap_copy(1, 1).wait_recv())
+            pl.when(gives == 1)(lambda: swap_copy(2).wait_recv())
         top = right.at[level, 0, 1 - level]
         bottom = right.at[level, 0, level]
 
@@ -174,7 +177,8 @@
         def _():
             base[...] = left[...]
 
-        pending = list(range(1, reach + 1))
+        pending = list(range(max(reach - lead, 1), reach + 1))
+        last = [pending.pop()] if split else []
         early = max(len(pending) // 4, 1)
 
         def some():
@@ -197,31 +201,80 @@
         def _():
             base[...] = mid[...]
 
-        while pending:
-            step(pending.pop(0))
-        settle(level, 1, second, None if level == 0 else "gives")
         mine = right.at[level, 1, core]
         theirs = right.at[level, 1, 1 - core]
         diag_factor, side_factor = (mine, theirs) if level == 0 else (theirs, mine)
-        product(base, diag_factor, keep_sum(outs[0], add))
-        after_diag()
-        product(front, side_factor, keep(outs[1]))
-
-    merge(0, first_ref, second_ref, left_ref, add_ref,
-          (swap.at[slot, 0], swap.at[slot, 1]), lambda: swap_copy(0, slot).start())
-    pl.when(gives == 0)(lambda: swap_copy(1, 1).start())
-    swap_copy(0, gives).wait_recv()
+        while pending:
+            step(pending.pop(0))
+        settle(level, 1, range(reach if split else reach + 1))
+        run(lambda guard: local_copy(level, 1, second).wait())
+
+        def term(left, factor, cols, p):
+            span = pl.ds(pl.multiple_of(p * rows, rows), rows)
+            return jnp.dot(left[:, span], factor[span, cols], preferred_element_type=jnp.float32)
+
+        near = [0] + [way * distance for distance in range(1, reach) for way in (1, -1)]
+
+        def partial(left, factor, out):
+            @pl.loop(0, width // TILE)
+            def _(tile):
+                cols = pl.ds(pl.multiple_of(tile * TILE, TILE), TILE)
+                out[:, cols] = sum(term(left, factor, cols, at_ring(shift)) for shift in near)
+
+        def finish(left, factor, part, emit):
+            @pl.loop(0, width // TILE)
+            def _(tile):
+                cols = pl.ds(pl.multiple_of(tile * TILE, TILE), TILE)
+                emit(cols, part[:, cols] + term(left, factor, cols, at_ring(reach)))
+
+        if split:
+            partial(base, diag_factor, sums.at[0])
+            partial(front, side_factor, sums.at[1])
+            step(last[0])
+            settle(level, 1, [reach])
+        if level == 1:
+            pl.when(gives == 1)(lambda: swap_copy(3).wait_recv())
+        if split:
+            finish(base, diag_factor, sums.at[0], keep_sum(outs[0], add))
+            after_diag()
+            finish(front, side_factor, sums.at[1], keep(outs[1]))
+        else:
+            product(base, diag_factor, keep_sum(outs[0], add))
+            after_diag()
+            product(front, side_factor, keep(outs[1]))
+
+    def give():
+        for half in range(2):
+            swap_copy(half).start()
+        open_ring(1, 0, swap.at[0, 0], "gives")
+
+    def take():
+        swap_copy(2).start()
+        open_ring(1, 0, swap.at[0, 0], "takes", lambda half: swap_copy(half).wait_recv())
+        swap_copy(3).start()
+
+    merge(0, max(reach - 1, 1), first_ref, second_ref, left_ref, add_ref,
+          (swap.at[slot, 0], swap.at[slot, 1]), lambda: pl.when(gives == 1)(give))
+    pl.when(gives == 0)(take)
 
     def last_copy(kind):
         return pltpu.make_async_remote_copy(
             src_ref=own_ref.at[kind], dst_ref=other_ref.at[kind], send_sem=last_send.at[kind],
             recv_sem=last_recv.at[kind], device_id=(sibling, panel), device_id_type=MESH)
 
-    merge(1, swap.at[0, 0], swap.at[0, 1], swap.at[1, 1], swap.at[1, 0],
+    merge(1, 1, swap.at[0, 0], swap.at[0, 1], swap.at[1, 1], swap.at[1, 0],
           (own_ref.at[0], own_ref.at[1]), lambda: last_copy(0).start())
     last_copy(1).start()
-    swap_copy(0, slot).wait_send()
-    pl.when(gives == 0)(lambda: swap_copy(1, 1).wait_send())
+
+    @pl.when(gives == 1)
+    def _():
+        for which in (0, 1):
+            swap_copy(which).wait_send()
+
+    @pl.when(gives == 0)
+    def _():
+        for which in (2, 3):
+            swap_copy(which).wait_send()
 
     def drain(guard):
         own = right.at[0, 0, 0, pl.ds(0, piece), :]
@@ -261,7 +314,7 @@
 
     outer = min(4, panels)
     inner = panels // outer
-    counts = 20 * panels
+    counts = 24 * panels
     vmem = pl.BlockSpec(memory_space=pltpu.VMEM)
     own, other = pl.pallas_call(
         functools.partial(kernel, outer, inner, counts),
@@ -271,13 +324,14 @@
         scratch_shapes=[
             pltpu.VMEM((2, 2, 2, width, width), jnp.bfloat16),
             pltpu.VMEM((2, 2, rows, width), jnp.bfloat16),
+            pltpu.VMEM((2, rows, width), jnp.float32),
             pltpu.VMEM((rows, width), jnp.bfloat16),
             pltpu.VMEM((rows, width), jnp.bfloat16),
             pltpu.VMEM((rows, width), jnp.bfloat16),
             pltpu.SemaphoreType.DMA((2, 2, 2, panels, 2)),
             pltpu.SemaphoreType.DMA((counts,)),
-            pltpu.SemaphoreType.DMA((2,)),
-            pltpu.SemaphoreType.DMA((2,)),
+            pltpu.SemaphoreType.DMA((4,)),
+            pltpu.SemaphoreType.DMA((4,)),
             pltpu.SemaphoreType.DMA((2, 2)),
             pltpu.SemaphoreType.DMA((2,)),
             pltpu.SemaphoreType.DMA((2,)),

time: 120 us -> 117 us (0.975); the launches traced: 118 us -> 117 us
    pallas_call x1, Pallas kernels: 114 us -> 113 us  [body(): pl.pallas_call(functools.partial(kernel, outer, inner, counts), out_shape...]
where the time goes in v3:
time: 117 us
  Pallas kernels  113 us (97%)
  matrix products  2.3 us (2%)
  other arithmetic  1.76 us (2%)
    pallas_call x1, Pallas kernels, body(): pl.pallas_call(functools.partial(kernel, outer, inner, counts), out_shape...  113 us

profile of v3, /device:TPU:0, one launch (start us, length us, event | category | flops | bytes accessed | tf_op | source)
XLA Modules:
  0.0 116.8 jit_solution(16512854666117067622)
XLA Ops:
  0.0 2.3 %fusion.17 = (bf16[4,128,1024]{2,1,0:T(8,128)(2,1)S(1)}, f32[4,128,1024]{2,1,0:T(8,128)S(1)}) fusion(s32[1024]{0:T(1024)S(1)} %add_select_fusion, s32[1,4,16,16]{3,2,1,0:T(8,128)} %param.3, s32[128]{0:T(128)S(1)} %and_select_fusion, f32[1,4,128,1024]{3,2,1,0:T(8,128)} %param.2), kind=kOutput, calls=%fused_computation.32 | convolution fusion | flops 18107392 | bytes 5251584 | tf_op jit(solution)/shard_map/mi,gij,jc->gmc/dot_general | solution.py:306
  2.3 0.1 select_bitcast_fusion
  2.4 0.1 fusion.add_ref
  2.5 112.7 %merge_levels.1 = (f32[2,128,1024]{2,1,0:T(8,128)S(1)}, f32[2,128,1024]{2,1,0:T(8,128)S(1)}) custom-call(bf16[128,1024]{1,0:T(8,128)(2,1)S(1)} %get-tuple-element.15.first_ref, bf16[128,1024]{1,0:T(8,128)(2,1)S(1)} %get-tuple-element.14.second_ref, bf16[128,1024]{1,0:T(8,128)(2,1)S(1)} %get-tuple-element.13.left_ref, f32[128,1024]{1,0:T(8,128)S(1)} %fusion.add_ref), custom_call_target="tpu_custom_call" | custom-call | tf_op jit(solution)/shard_map/merge_levels/pallas_call | solution.py:319
  115.2 0.2 slice_select_fusion.4
  115.4 1.5 %maximum_bitcast_fusion = f32[1,4,128,1024]{3,2,1,0:T(8,128)} fusion(f32[1,128,1024]{2,1,0:T(8,128)S(1)} %get-tuple-element.10, f32[1,128,1024]{2,1,0:T(8,128)S(1)} %get-tuple-element.11, f32[1,128,1024]{2,1,0:T(8,128)S(1)} %get-tuple-element.12, f32[1,128,1024]{2,1,0:T(8,128)S(1)} %get-tuple-element.9), kind=kLoop, calls=%fused_computation | loop fusion | flops 1572864 | bytes 4194304 | tf_op jit(solution)/shard_map/broadcast_in_dim | solution.py:343
  (2 shorter events, 0.0 us)

commit v4 on v3

--- a/solution.py
+++ b/solution.py
@@ -7,7 +7,6 @@
 from jax.sharding import PartitionSpec as P
 
 BLK = 64
-TILE = 256
 MESH = pl.DeviceIdType.MESH
 
 
@@ -115,9 +114,9 @@
     slot = 1 - gives
 
     def product(left, factor, emit):
-        @pl.loop(0, width // TILE)
+        @pl.loop(0, width // width)
         def _(step):
-            cols = pl.ds(pl.multiple_of(step * TILE, TILE), TILE)
+            cols = pl.ds(pl.multiple_of(step * width, width), width)
             emit(cols, jnp.dot(left[...], factor[:, cols], preferred_element_type=jnp.float32))
 
     def keep(ref):
@@ -150,15 +149,20 @@
             if level == 1:
                 pl.when(gives == 0)(lambda: follow(level, 1, distance))
 
+        def start_second():
+            run(lambda guard: open_ring(level, 1, second, guard))
+            if level == 1:
+                pl.when(gives == 0)(lambda: follow(level, 1, 0))
+
         split = rows % 128 == 0
         if level == 0:
             open_ring(level, 0, first)
+        if lead == 0:
+            start_second()
         for distance in range(1, reach):
             relay(level, 0, distance)
             if distance == lead:
-                run(lambda guard: open_ring(level, 1, second, guard))
-                if level == 1:
-                    pl.when(gives == 0)(lambda: follow(level, 1, 0))
+                start_second()
             if distance > lead:
                 step(distance - lead)
         relay(level, 0, reach)
@@ -216,15 +220,15 @@
         near = [0] + [way * distance for distance in range(1, reach) for way in (1, -1)]
 
         def partial(left, factor, out):
-            @pl.loop(0, width // TILE)
+            @pl.loop(0, width // width)
             def _(tile):
-                cols = pl.ds(pl.multiple_of(tile * TILE, TILE), TILE)
+                cols = pl.ds(pl.multiple_of(tile * width, width), width)
                 out[:, cols] = sum(term(left, factor, cols, at_ring(shift)) for shift in near)
 
         def finish(left, factor, part, emit):
-            @pl.loop(0, width // TILE)
+            @pl.loop(0, width // width)
             def _(tile):
-                cols = pl.ds(pl.multiple_of(tile * TILE, TILE), TILE)
+                cols = pl.ds(pl.multiple_of(tile * width, width), width)
                 emit(cols, part[:, cols] + term(left, factor, cols, at_ring(reach)))
 
         if split:
@@ -253,7 +257,7 @@
         open_ring(1, 0, swap.at[0, 0], "takes", lambda half: swap_copy(half).wait_recv())
         swap_copy(3).start()
 
-    merge(0, max(reach - 1, 1), first_ref, second_ref, left_ref, add_ref,
+    merge(0, 1, first_ref, second_ref, left_ref, add_ref,
           (swap.at[slot, 0], swap.at[slot, 1]), lambda: pl.when(gives == 1)(give))
     pl.when(gives == 0)(take)
 
@@ -262,7 +266,7 @@
             src_ref=own_ref.at[kind], dst_ref=other_ref.at[kind], send_sem=last_send.at[kind],
             recv_sem=last_recv.at[kind], device_id=(sibling, panel), device_id_type=MESH)
 
-    merge(1, 1, swap.at[0, 0], swap.at[0, 1], swap.at[1, 1], swap.at[1, 0],
+    merge(1, 0, swap.at[0, 0], swap.at[0, 1], swap.at[1, 1], swap.at[1, 0],
           (own_ref.at[0], own_ref.at[1]), lambda: last_copy(0).start())
     last_copy(1).start()
 

time: 117 us -> 101 us (0.86)
  Pallas kernels: 113 us -> 96.6 us
    pallas_call x1, Pallas kernels: 113 us -> 96.6 us  [body(): pl.pallas_call(functools.partial(kernel, outer, inner, counts), out_shape...]
where the time goes in v4:
time: 101 us
  Pallas kernels  96.6 us (96%)
  matrix products  2.3 us (2%)
  other arithmetic  1.76 us (2%)
    pallas_call x1, Pallas kernels, body(): pl.pallas_call(functools.partial(kernel, outer, inner, counts), out_shape...  96.6 us
    dot_general x1, matrix products, body(): jnp.einsum('mi,gij,jc->gmc', row_pick, pattern[0].astype(jnp.float32), co...  2.3 us

profile of v4, /device:TPU:0, one launch (start us, length us, event | category | flops | bytes accessed | tf_op | source)
XLA Modules:
  0.0 100.7 jit_solution(11441111671285838568)
XLA Ops:
  0.0 2.3 %fusion.17 = (bf16[4,128,1024]{2,1,0:T(8,128)(2,1)S(1)}, f32[4,128,1024]{2,1,0:T(8,128)S(1)}) fusion(s32[1024]{0:T(1024)S(1)} %add_select_fusion, s32[1,4,16,16]{3,2,1,0:T(8,128)} %param.3, s32[128]{0:T(128)S(1)} %and_select_fusion, f32[1,4,128,1024]{3,2,1,0:T(8,128)} %param.2), kind=kOutput, calls=%fused_computation.32 | convolution fusion | flops 18107392 | bytes 5251584 | tf_op jit(solution)/shard_map/mi,gij,jc->gmc/dot_general | solution.py:310
  2.3 0.1 select_bitcast_fusion
  2.4 0.1 fusion.add_ref
  2.5 96.6 %merge_levels.1 = (f32[2,128,1024]{2,1,0:T(8,128)S(1)}, f32[2,128,1024]{2,1,0:T(8,128)S(1)}) custom-call(bf16[128,1024]{1,0:T(8,128)(2,1)S(1)} %get-tuple-element.15.first_ref, bf16[128,1024]{1,0:T(8,128)(2,1)S(1)} %get-tuple-element.14.second_ref, bf16[128,1024]{1,0:T(8,128)(2,1)S(1)} %get-tuple-element.13.left_ref, f32[128,1024]{1,0:T(8,128)S(1)} %fusion.add_ref), custom_call_target="tpu_custom_call" | custom-call | tf_op jit(solution)/shard_map/merge_levels/pallas_call | solution.py:323
  99.0 0.2 slice_select_fusion.4
  99.2 1.5 %maximum_bitcast_fusion = f32[1,4,128,1024]{3,2,1,0:T(8,128)} fusion(f32[1,128,1024]{2,1,0:T(8,128)S(1)} %get-tuple-element.10, f32[1,128,1024]{2,1,0:T(8,128)S(1)} %get-tuple-element.11, f32[1,128,1024]{2,1,0:T(8,128)S(1)} %get-tuple-element.12, f32[1,128,1024]{2,1,0:T(8,128)S(1)} %get-tuple-element.9), kind=kLoop, calls=%fused_computation | loop fusion | flops 1572864 | bytes 4194304 | tf_op jit(solution)/shard_map/broadcast_in_dim | solution.py:347
  (2 shorter events, 0.0 us)
